TPU v7x, 512 devices: a whole 4x8x8 slice. The times are simulated.
512 devices in a mesh: group: 8 (over x, z_lo), shard: 64 (over z_hi, y, core).
Axes of the slice: x: 4, y: 8, z: 8 (z_hi: 4, z_lo: 2; z = z_hi * 2 + z_lo), core: 2. Of those that a mesh axis runs over, the one named last changes fastest.
Arguments:
- tokens: bfloat16 [512, 3072], P('group', 'shard'), may hold values from -6 to 6
- cotangent: bfloat16 [512, 3072], P('group', 'shard'), may hold values from -1.5 to 1.5
- expert_ids: int32 [512, 2], P('group'), may hold values from 0 to 7, all different within a row; in each aligned block of 64 rows (0 to 63, 64 to 127, ...) at most 36 rows name the same one
- route_weight: float32 [512, 2], P('group'), may hold values from 0.1 to 0.9
- w_gate: bfloat16 [8, 3072, 8192], P('group', None, 'shard'), may hold values from -0.109375 to 0.109375
- w_up: bfloat16 [8, 3072, 8192], P('group', None, 'shard'), may hold values from -0.109375 to 0.109375
- w_down: bfloat16 [8, 8192, 3072], P('group', 'shard'), may hold values from -0.109375 to 0.109375
Outputs:
- grad_tokens: bfloat16 [512, 3072], P('group', 'shard')
- grad_gate: bfloat16 [8, 3072, 8192], P('group', None, 'shard')
- grad_up: bfloat16 [8, 3072, 8192], P('group', None, 'shard')
Inputs may be any that keep to these rules, and one draw needn't show every extreme that they name: `expert_ids`: each token names 2 different experts. Among the 64 tokens of one aligned block (the tokens of one index of group), no expert is named by more than 36 tokens.
All inputs are finite; a program needn't handle non-finite values.
Results may differ from a plain program's by a relative error of at most 0.0064.
Values may be sent and summed in bfloat16 or wider, within the bound.
A program may use at most 64 MiB of HBM per device.

v0:
```python
import jax
import jax.numpy as jnp
from jax import lax
from jax.sharding import PartitionSpec as P

EXPERTS = 8
CAP = 36
exact_mode = lax.Precision.HIGHEST


def slot_table(expert_ids, capacity):
    experts_axis = jnp.arange(EXPERTS, dtype=jnp.int32)
    counted = jnp.sum(
        (expert_ids[:, :, None] == experts_axis[None, None, :]).astype(jnp.int32), axis=1
    )
    ranking = jnp.cumsum(counted, axis=0) - 1
    places = jnp.arange(capacity, dtype=jnp.int32)
    slot_map = (counted.T[:, None, :] == 1) & (ranking.T[:, None, :] == places[None, :, None])
    return (counted, slot_map)


def slot_scales(slot_map, expert_ids, route_weight):
    experts_axis = jnp.arange(EXPERTS, dtype=jnp.int32)
    per_expert = jnp.sum(
        jnp.where(
            expert_ids[:, :, None] == experts_axis[None, None, :],
            route_weight[:, :, None],
            jnp.float32(0.0),
        ),
        axis=1,
    )
    return jnp.einsum("ect,te->ec", slot_map.astype(jnp.float32), per_expert, precision=exact_mode)


def place_rows(slot_map, scales, inputs, cotangents):
    selector = slot_map.astype(jnp.bfloat16)
    picked_inputs = jnp.einsum(
        "ect,td->ecd", selector, inputs, preferred_element_type=jnp.float32
    ).astype(jnp.bfloat16)
    picked_cot = jnp.einsum("ect,td->ecd", selector, cotangents, preferred_element_type=jnp.float32)
    scaled_cot = (scales[:, :, None] * picked_cot).astype(jnp.bfloat16)
    return (picked_inputs, scaled_cot)


def slot_grads(slot_inputs, slot_cotangents, paired, down_weight):
    hidden_width = down_weight.shape[0]
    joined = jnp.dot(slot_inputs, paired, preferred_element_type=jnp.float32)
    gate_pre = joined[:, :hidden_width]
    up_value = joined[:, hidden_width:]
    sigmoid_gate = jax.nn.sigmoid(gate_pre)
    active = gate_pre * sigmoid_gate
    hidden_grad = lax.dot_general(
        slot_cotangents, down_weight, (((1,), (1,)), ((), ())), preferred_element_type=jnp.float32
    )
    gate_grad = (
        hidden_grad * up_value * sigmoid_gate * (1.0 + gate_pre * (1.0 - sigmoid_gate))
    ).astype(jnp.bfloat16)
    up_grad = (hidden_grad * active).astype(jnp.bfloat16)
    stacked = jnp.concatenate([gate_grad, up_grad], axis=1)
    input_grad = lax.dot_general(
        stacked, paired, (((1,), (1,)), ((), ())), preferred_element_type=jnp.float32
    )
    return (input_grad, stacked)


def source_partials(slot_inputs, stacked, sources):
    capacity = slot_inputs.shape[0] // sources

    def accumulate(source, running):
        begin = (source * capacity).astype(jnp.int32)
        piece_inputs = lax.dynamic_slice_in_dim(slot_inputs, begin, capacity, 0)
        piece_grads = lax.dynamic_slice_in_dim(stacked, begin, capacity, 0)
        partial_sum = lax.dot_general(
            piece_inputs, piece_grads, (((0,), (0,)), ((), ())), preferred_element_type=jnp.float32
        )
        return running + lax.optimization_barrier(partial_sum.astype(jnp.bfloat16)).astype(
            jnp.float32
        )

    initial = jnp.zeros((slot_inputs.shape[1], stacked.shape[1]), jnp.float32)
    return lax.fori_loop(jnp.int32(0), jnp.int32(sources), accumulate, initial)


def body(tokens, cotangent, expert_ids, route_weight, w_gate, w_up, w_down):
    groups = lax.axis_size("group")
    hidden_width = w_gate.shape[2]
    counted, slot_map = slot_table(expert_ids, CAP)
    scales = slot_scales(slot_map, expert_ids, route_weight)
    paired_local = jnp.concatenate([w_gate, w_up], axis=2)
    sent_inputs, sent_cot = place_rows(slot_map, scales, tokens, cotangent)
    part_inputs, part_cot = (
        lax.all_to_all(sent_inputs, "group", split_axis=0, concat_axis=1, tiled=True),
        lax.all_to_all(sent_cot, "group", split_axis=0, concat_axis=1, tiled=True),
    )
    slot_inputs, slot_cot = (
        lax.all_gather(part_inputs, "shard", axis=2, tiled=True),
        lax.all_gather(part_cot, "shard", axis=2, tiled=True),
    )
    input_grad, stacked = slot_grads(slot_inputs[0], slot_cot[0], paired_local[0], w_down[0])
    grads_rows = [input_grad]
    weight_totals = [source_partials(slot_inputs[0], stacked, groups)]
    slot_grad = jnp.stack(grads_rows)
    summed_rows = lax.psum_scatter(slot_grad, "shard", scatter_dimension=2, tiled=True)
    returned = lax.all_to_all(summed_rows, "group", split_axis=1, concat_axis=0, tiled=True)
    grad_total = jnp.einsum(
        "ect,ecd->td", slot_map.astype(jnp.float32), returned, precision=exact_mode
    )
    stacked_totals = jnp.stack(weight_totals)
    grad_gate = stacked_totals[:, :, :hidden_width].astype(jnp.bfloat16)
    grad_up = stacked_totals[:, :, hidden_width:].astype(jnp.bfloat16)
    return (grad_total.astype(jnp.bfloat16), grad_gate, grad_up)


def solution(mesh):
    in_specs = (
        P("group", "shard"),
        P("group", "shard"),
        P("group", None),
        P("group", None),
        P("group", None, "shard"),
        P("group", None, "shard"),
        P("group", "shard", None),
    )
    out_specs = (P("group", "shard"), P("group", None, "shard"), P("group", None, "shard"))
    return jax.shard_map(body, mesh=mesh, in_specs=in_specs, out_specs=out_specs, check_vma=False)
```

profile of v0, /device:TPU:1, one launch (start us, length us, event | category | flops | bytes accessed | tf_op | source)
XLA Modules:
  0.0 811.4 jit_solution(8384122965178680824)
XLA Ops:
  7.2 0.8 convert_reduce_fusion
  8.2 0.9 convolution_convert_fusion.1
  9.3 11.5 %all_to_all.36 = bf16[8,2,864]{2,1,0:T(2,128)(2,1)S(1)} all-to-all(bf16[8,2,864]{2,1,0:T(2,128)(2,1)S(1)} %reshape.42), channel_id=1, replica_groups=mesh['group'=8,'shard'=64] {'group'}, dimensions={0} | all-to-all | bytes 55296 | tf_op jit(solution)/shard_map/all_to_all | solution.py:92
  21.0 0.7 copy.46
  21.7 0.7 select_reduce_fusion
  22.5 0.2 fusion.13
  22.7 0.9 fusion.5
  23.7 7.5 all_to_all.37
  31.3 0.7 copy.45
  32.1 1.3 dynamic-slice
  34.1 76.7 %all-gather.5.cloned.1.call-done = bf16[1,288,3072]{1,2,0:T(8,128)(2,1)} async-done(((bf16[1,288,48]{1,2,0:T(8,128)(2,1)}), bf16[1,288,3072]{1,2,0:T(8,128)(2,1)}) %all-gather.5.cloned.1.call-update) | async-done | bytes 1769488 | tf_op jit(solution)/shard_map/all_gather | solution.py:96
  110.8 2.9 fusion.7
  113.7 82.8 %all-gather.3.cloned.1.call-done = bf16[1,288,3072]{1,2,0:T(8,128)(2,1)} async-done(((bf16[1,288,48]{1,2,0:T(8,128)(2,1)}), bf16[1,288,3072]{1,2,0:T(8,128)(2,1)}) %all-gather.3.cloned.1.call-update) | async-done | bytes 1769488 | tf_op jit(solution)/shard_map/all_gather | solution.py:97
  196.5 2.7 fusion.17
  199.2 2.4 convolution_bitcast_fusion
  201.6 2.4 copy.42
  204.0 10.6 %copy.38 = f32[1,288,3072]{1,0,2:T(1,128)} copy(f32[1,288,3072]{2,1,0:T(8,128)} %convolution_bitcast_fusion) | data formatting | bytes 7077888 | tf_op jit(solution)/shard_map/stack | solution.py:102
  214.7 41.6 %while.11 = (s32[]{:T(128)}, f32[3072,256]{1,0:T(8,128)}, bf16[288,3072]{1,0:T(8,128)(2,1)}, bf16[288,256]{1,0:T(8,128)(2,1)S(1)}, s32[]{:T(128)}, /*index=5*/s32[]{:T(128)}, s32[]{:T(128)}, s32[]{:T(128)}) while((s32[]{:T(128)}, f32[3072,256]{1,0:T(8,128)}, bf16[288,3072]{1,0:T(8,128)(2,1)}, bf16[288,256]{1,0:T(8,128)(2,1)S(1)}, ...), condition=%wide.region_5.6_spmd.clone, body=%wide.region_4.5_spmd.clone.sunk | while | flops 59768836 | bytes 9704589 | solution.py:81
  214.7 1.6 convolution_convert_fusion.3
  216.3 1.9 select_add_fusion.2
  218.2 1.6 convolution_convert_fusion.3
  219.8 3.8 select_add_fusion.2
  223.7 1.6 convolution_convert_fusion.3
  225.3 3.8 select_add_fusion.2
  229.1 1.6 convolution_convert_fusion.3
  230.7 3.8 select_add_fusion.2
  234.5 1.6 convolution_convert_fusion.3
  236.1 3.9 select_add_fusion.2
  240.0 1.6 convolution_convert_fusion.3
  241.6 3.8 select_add_fusion.2
  245.4 1.6 convolution_convert_fusion.3
  247.0 3.8 select_add_fusion.2
  250.8 1.6 convolution_convert_fusion.3
  252.4 3.9 select_add_fusion.2
  256.3 2.0 convert_bitcast_fusion
  258.3 530.2 %all-reduce.3.cloned.1.call-done = f32[1,288,3072]{1,0,2:T(1,128)} async-done(((f32[1,288,3072]{1,0,2:T(1,128)}), f32[1,288,3072]{1,0,2:T(1,128)}) %all-reduce.3.cloned.1.call-update) | async-done | bytes 3538960
  788.6 0.9 constant_dynamic-slice_fusion
  789.6 0.5 broadcast.32
  790.1 1.0 reduce.5
  791.1 0.8 reshape.44
  791.9 4.2 all-to-all-start.2
  796.1 1.2 fusion.31
  797.3 4.0 all-to-all-done.2
  801.3 0.8 reduce.6
  802.1 0.3 reshape.45
  802.4 0.5 broadcast.31
  802.9 1.0 bitcast_reduce_fusion
  804.0 0.9 fusion.6
  (29 shorter events, 1.2 us)
Async XLA Ops:
  7.2 189.3 %copy-start = (bf16[1,128,3072]{2,1,0:T(8,128)(2,1)S(1)}, bf16[1,128,3072]{2,1,0:T(8,128)(2,1)}, u32[]{:S(2)}) copy-start(bf16[1,128,3072]{2,1,0:T(8,128)(2,1)} %param.15) | copy-start | bytes 2359300
  7.2 103.6 %all-gather.5.cloned.1.call-start = ((), (), s32[]{:S(2)}) async-start(), calls=%async_computation.4 | async-start | bytes 2396160 | tf_op jit(solution)/shard_map/all_gather | solution.py:96
  21.7 174.8 %all-gather.3.cloned.1.call-start = ((), (), s32[]{:S(2)}) async-start(), calls=%async_computation.3 | async-start | bytes 2396160 | tf_op jit(solution)/shard_map/all_gather | solution.py:97
  32.1 756.5 %all-reduce.3.cloned.1.call-start = ((), (), s32[]{:S(2)}) async-start(), calls=%async_computation.5 | async-start | bytes 9437184
  196.5 2.7 copy-start.2
  196.5 2.7 copy-start.3
  199.2 2.4 copy-start.1
  791.9 9.4 %all-to-all-start.2 = ((f32[8,1,1728]{2,1,0:T(1,128)}), f32[8,1,1728]{2,1,0:T(1,128)S(1)}, u32[]{:S(2)}, u32[]{:S(2)}) async-start(f32[8,1,1728]{2,1,0:T(1,128)} %reshape.44), calls=%async_computation.2 | async-start | bytes 114688 | tf_op jit(solution)/shard_map/all_to_all | solution.py:104
Sparse Core Ops, SparseCore 0:
  21.8 88.8 all-gather.4
  114.5 81.9 all-gather.2
  214.8 573.7 all-reduce.2
where the time goes:
time: 813 us; the launch traced here: 811 us
  waiting for transfers between devices  694 us (85%)
  other arithmetic  34.2 us (4%)
  matrix products  23.6 us (3%)
  local copies, waits for them, and re-layouts  21.8 us (3%)
  blocking collectives  19 us (2%)
  between operations  14.6 us (2%)
    unnamed x4, waiting for transfers between devices  530 us
    all_gather x1, waiting for transfers between devices, body(): lax.all_gather(part_cot, 'shard', axis=2, tiled=True)  82.8 us
    all_gather x1, waiting for transfers between devices, body(): lax.all_gather(part_inputs, 'shard', axis=2, tiled=True)  76.7 us
    add x8, other arithmetic, accumulate(): running + lax.optimization_barrier(partial_sum.astype(jnp.bfloat16)).asty...  28.8 us
  transfers between devices with their start and end apart: 4, of which 4 were waited for; matrix products, arithmetic and copies ran while one was open for 6% of the time, Pallas kernels for 0%

commit v1 on v0

--- a/solution.py
+++ b/solution.py
@@ -94,7 +94,9 @@
     )
     slot_inputs, slot_cot = (
         lax.all_gather(part_inputs, "shard", axis=2, tiled=True),
-        lax.all_gather(part_cot, "shard", axis=2, tiled=True),
+        jnp.concatenate(
+            lax.all_to_all(jnp.stack([part_cot] * lax.axis_size("shard")), "shard", 0, 0), axis=2
+        ),
     )
     input_grad, stacked = slot_grads(slot_inputs[0], slot_cot[0], paired_local[0], w_down[0])
     grads_rows = [input_grad]

time: 813 us -> 773 us (0.951)
  waiting for transfers between devices: 694 us -> 638 us
  starting transfers between devices: 4.29 us -> 29.4 us
  blocking collectives: 19 us -> 7.46 us
    all_gather x1 -> x0, waiting for transfers between devices: 82.8 us -> none  [body(): lax.all_gather(part_cot, 'shard', axis=2, tiled=True)]
    all_to_all x0 -> x2, starting transfers between devices: none -> 25.1 us  [the longest x1 18.5 us: body(): lax.all_to_all(jnp.stack([part_cot] * lax.axis_size('shard')), 'shard', 0...]
    all_gather x1, waiting for transfers between devices: 76.7 us -> 99.4 us  [body(): lax.all_gather(part_inputs, 'shard', axis=2, tiled=True)]
    all_to_all x1 -> x0, blocking collectives: 11.5 us -> none  [body(): lax.all_to_all(sent_inputs, 'group', split_axis=0, concat_axis=1, tiled=T...]
    unnamed x4 -> x3, waiting for transfers between devices: 530 us -> 530 us
  transfers between devices with their start and end apart: 4 -> 5, of which waited for: 4 -> 4; matrix products, arithmetic and copies ran while one was open for 6% -> 7% of each run, Pallas kernels for 0% -> 0%
where the time goes in v1:
time: 773 us; the launch traced here: 771 us
  waiting for transfers between devices  638 us (83%)
  other arithmetic  34.2 us (4%)
  starting transfers between devices  29.4 us (4%)
  matrix products  23.6 us (3%)
  local copies, waits for them, and re-layouts  23.4 us (3%)
  between operations  14.9 us (2%)
    unnamed x3, waiting for transfers between devices  530 us
    all_gather x1, waiting for transfers between devices, body(): lax.all_gather(part_inputs, 'shard', axis=2, tiled=True)  99.4 us
    add x8, other arithmetic, accumulate(): running + lax.optimization_barrier(partial_sum.astype(jnp.bfloat16)).asty...  28.8 us
    all_to_all x1, starting transfers between devices, body(): lax.all_to_all(jnp.stack([part_cot] * lax.axis_size('shard')), 'shard', 0...  18.5 us
  transfers between devices with their start and end apart: 5, of which 4 were waited for; matrix products, arithmetic and copies ran while one was open for 7% of the time, Pallas kernels for 0%

profile of v1, /device:TPU:1, one launch (start us, length us, event | category | flops | bytes accessed | tf_op | source)
XLA Modules:
  0.0 771.0 jit_solution(11267570977507420075)
XLA Ops:
  7.2 0.8 convert_reduce_fusion
  8.2 0.9 convolution_convert_fusion.1
  9.1 0.7 reshape.51
  9.8 6.6 all-to-all-start.2
  16.5 0.7 select_reduce_fusion
  17.2 4.3 all-to-all-done.2
  21.7 0.7 copy.46
  22.7 0.9 fusion.3
  23.7 7.5 all_to_all.38
  31.5 1.6 stack.9
  33.1 18.5 %all-to-all-start.1 = ((bf16[64,1,288,48]{2,3,1,0:T(8,128)(2,1)}), bf16[64,1,288,48]{2,3,1,0:T(8,128)(2,1)S(1)}, u32[]{:S(2)}, u32[]{:S(2)}) async-start(bf16[64,1,288,48]{2,3,1,0:T(8,128)(2,1)} %stack.9), calls=%async_computation.1 | async-start | bytes 4718592 | tf_op jit(solution)/shard_map/all_to_all | solution.py:98
  51.6 1.3 dynamic-slice
  53.5 99.4 %all-gather.2.cloned.1.call-done = bf16[1,288,3072]{1,2,0:T(8,128)(2,1)} async-done(((bf16[1,288,48]{1,2,0:T(8,128)(2,1)}), bf16[1,288,3072]{1,2,0:T(8,128)(2,1)}) %all-gather.2.cloned.1.call-update) | async-done | bytes 1769488 | tf_op jit(solution)/shard_map/all_gather | solution.py:96
  152.9 3.6 fusion.5
  156.5 2.0 fusion.16
  158.6 2.4 convolution_bitcast_fusion
  161.0 2.4 copy.42
  163.4 10.6 %copy.38 = f32[1,288,3072]{1,0,2:T(1,128)} copy(f32[1,288,3072]{2,1,0:T(8,128)} %convolution_bitcast_fusion) | data formatting | bytes 7077888 | tf_op jit(solution)/shard_map/stack | solution.py:104
  174.0 41.6 %while.11 = (s32[]{:T(128)}, f32[3072,256]{1,0:T(8,128)}, bf16[288,3072]{1,0:T(8,128)(2,1)}, bf16[288,256]{1,0:T(8,128)(2,1)S(1)}, s32[]{:T(128)}, /*index=5*/s32[]{:T(128)}, s32[]{:T(128)}, s32[]{:T(128)}) while((s32[]{:T(128)}, f32[3072,256]{1,0:T(8,128)}, bf16[288,3072]{1,0:T(8,128)(2,1)}, bf16[288,256]{1,0:T(8,128)(2,1)S(1)}, ...), condition=%wide.region_5.6_spmd.clone, body=%wide.region_4.5_spmd.clone.sunk | while | flops 59768836 | bytes 9704589 | solution.py:81
  174.1 1.6 convolution_convert_fusion.3
  175.7 1.9 select_add_fusion.2
  177.6 1.6 convolution_convert_fusion.3
  179.2 3.8 select_add_fusion.2
  183.0 1.6 convolution_convert_fusion.3
  184.6 3.8 select_add_fusion.2
  188.5 1.6 convolution_convert_fusion.3
  190.1 3.8 select_add_fusion.2
  193.9 1.6 convolution_convert_fusion.3
  195.5 3.9 select_add_fusion.2
  199.4 1.6 convolution_convert_fusion.3
  201.0 3.8 select_add_fusion.2
  204.8 1.6 convolution_convert_fusion.3
  206.4 3.8 select_add_fusion.2
  210.2 1.6 convolution_convert_fusion.3
  211.8 3.9 select_add_fusion.2
  215.7 2.0 convert_bitcast_fusion
  217.7 530.2 %all-reduce.3.cloned.1.call-done = f32[1,288,3072]{1,0,2:T(1,128)} async-done(((f32[1,288,3072]{1,0,2:T(1,128)}), f32[1,288,3072]{1,0,2:T(1,128)}) %all-reduce.3.cloned.1.call-update) | async-done | bytes 3538960
  747.9 0.9 constant_dynamic-slice_fusion
  748.9 0.5 broadcast.34
  749.4 1.0 reduce.5
  750.4 0.8 reshape.53
  751.2 4.2 all-to-all-start.3
  755.4 1.2 fusion.30
  756.6 4.0 all-to-all-done.3
  760.7 0.8 reduce.6
  761.7 0.5 broadcast.33
  762.2 1.0 bitcast_reduce_fusion
  763.3 0.9 fusion.4
  (30 shorter events, 1.6 us)
Async XLA Ops:
  7.2 149.4 %copy-start = (bf16[1,128,3072]{2,1,0:T(8,128)(2,1)S(1)}, bf16[1,128,3072]{2,1,0:T(8,128)(2,1)}, u32[]{:S(2)}) copy-start(bf16[1,128,3072]{2,1,0:T(8,128)(2,1)} %param.15) | copy-start | bytes 2359300
  9.8 11.7 %all-to-all-start.2 = ((bf16[8,2,864]{2,1,0:T(2,128)(2,1)}), bf16[8,2,864]{2,1,0:T(2,128)(2,1)S(1)}, u32[]{:S(2)}, u32[]{:S(2)}) async-start(bf16[8,2,864]{2,1,0:T(2,128)(2,1)} %reshape.51), calls=%async_computation.2 | async-start | bytes 57344 | tf_op jit(solution)/shard_map/all_to_all | solution.py:92
  16.5 136.4 %all-gather.2.cloned.1.call-start = ((), (), s32[]{:S(2)}) async-start(), calls=%async_computation.4 | async-start | bytes 2396160 | tf_op jit(solution)/shard_map/all_gather | solution.py:96
  33.1 123.5 %all-to-all-start.1 = ((bf16[64,1,288,48]{2,3,1,0:T(8,128)(2,1)}), bf16[64,1,288,48]{2,3,1,0:T(8,128)(2,1)S(1)}, u32[]{:S(2)}, u32[]{:S(2)}) async-start(bf16[64,1,288,48]{2,3,1,0:T(8,128)(2,1)} %stack.9), calls=%async_computation.1 | async-start | bytes 4718592 | tf_op jit(solution)/shard_map/all_to_all | solution.py:98
  51.5 696.3 %all-reduce.3.cloned.1.call-start = ((), (), s32[]{:S(2)}) async-start(), calls=%async_computation.5 | async-start | bytes 9437184
  156.5 2.0 copy-start.2
  156.5 2.0 copy-start.3
  158.6 2.4 copy-start.1
  751.2 9.4 %all-to-all-start.3 = ((f32[8,1,1728]{2,1,0:T(1,128)}), f32[8,1,1728]{2,1,0:T(1,128)S(1)}, u32[]{:S(2)}, u32[]{:S(2)}) async-start(f32[8,1,1728]{2,1,0:T(1,128)} %reshape.53), calls=%async_computation.3 | async-start | bytes 114688 | tf_op jit(solution)/shard_map/all_to_all | solution.py:106
Sparse Core Ops, SparseCore 0:
  22.6 130.2 all-gather.1
  174.2 573.6 all-reduce.2
